TPU v7x, 32 devices: a whole 2x2x4 slice. The times are simulated.
32 devices in a mesh: grp: 2 (over y), date: 4 (over z), row: 4 (over x, core).
Axes of the slice: x: 2, y: 2, z: 4, core: 2. Of those that a mesh axis runs over, the one named last changes fastest.
Arguments:
- stack_data: float32 [16, 2, 64, 512], P(('grp', 'date'), None, 'row'), parts along dimension 0, may hold values from -40 to 40, as said below
- plan: int32 [8], replicated, may hold values from 0 to 7, each once
Outputs:
- coherence: float32 [16, 8, 2, 64, 512], P(('grp', 'date'), None, None, 'row'), parts along dimension 0
There are 2 independent parts, one for each index of `grp`. A program takes and returns all parts, laid end to end along the dimension named above; an argument that names none is the same for every part. Nothing has to cross between parts.
Inputs may be any that keep to these rules, and one draw needn't show every extreme that they name: `stack_data`: complex samples of one scene seen on every date, each date with its own phase, strength and noise.
All inputs are finite; a program needn't handle non-finite values.
Results may differ from a plain program's by a relative error of at most 0.00005.
Values sent between devices are 32-bit elements; how exact they have to be, the bound alone decides.
A program may use at most 64 MiB of HBM per device.

v0:
```python
import functools

import jax
import jax.numpy as jnp
from jax import lax
from jax.experimental import pallas as pl
from jax.experimental.pallas import tpu as pltpu
from jax.sharding import PartitionSpec as P

HALF_ROWS = 4
HALF_COLS = 16
LANES = 128

epsilon = 1e-06


def gather_kernel(n, rows_n, x_ref, coh, own, edge, mid, top, bot, mine, other, band, pbuf, sbuf, lhs, pw,
                  load_sem, recv, right_send, left_send, top_recv, bot_recv, down_send, up_send):
    local, _, height, width = x_ref.shape
    tiles = width // LANES
    inner = height - 2 * HALF_ROWS
    span = height + 2 * HALF_ROWS
    me = lax.axis_index("date")
    row = lax.axis_index("row")
    has_left, has_right = me > 0, me < n - 1
    at_end = jnp.logical_not(jnp.logical_and(has_left, has_right))
    has_up, has_down = row > 0, row < rows_n - 1

    load = pltpu.make_async_copy(x_ref, own, load_sem)
    load.start()
    barrier = pltpu.get_barrier_semaphore()

    def greet(axis, index):
        pl.semaphore_signal(barrier, inc=1, device_id={axis: index}, device_id_type=pl.DeviceIdType.MESH)

    pl.when(has_left)(lambda: greet("date", me - 1))
    pl.when(has_right)(lambda: greet("date", me + 1))
    pl.when(has_up)(lambda: greet("row", row - 1))
    pl.when(has_down)(lambda: greet("row", row + 1))

    col_in = lax.broadcasted_iota(jnp.int32, (width, width), 0)
    col_out = lax.broadcasted_iota(jnp.int32, (width, width), 1)
    band[...] = jnp.where(jnp.abs(col_in - col_out) <= HALF_COLS, 1.0, 0.0).astype(jnp.bfloat16)

    @pl.when(row == 0)
    def _():
        top[...] = jnp.zeros_like(top)

    @pl.when(row == rows_n - 1)
    def _():
        bot[...] = jnp.zeros_like(bot)

    def remote(src, dst, send_sem, recv_sem, axis, index):
        return pltpu.make_async_remote_copy(
            src_ref=src, dst_ref=dst, send_sem=send_sem, recv_sem=recv_sem,
            device_id={axis: index}, device_id_type=pl.DeviceIdType.MESH)

    chunks = [(0, l) for l in range(local)] + [(1, l) for l in range(local)]

    def to_date(sends, step, k, s, l):
        ref = (edge, mid)[k].at[s, l]
        return remote(ref, ref, sends.at[k, s, l], recv.at[k, s, l], "date", me + step)

    def to_right(k, s, l):
        return to_date(right_send, 1, k, s, l)

    def to_left(k, s, l):
        return to_date(left_send, -1, k, s, l)

    def to_down(s, l):
        return remote(edge.at[s, l, 1], top.at[s, l], down_send.at[s, l], top_recv.at[s, l], "row", row + 1)

    def to_up(s, l):
        return remote(edge.at[s, l, 0], bot.at[s, l], up_send.at[s, l], bot_recv.at[s, l], "row", row - 1)

    def send_rims(s, l):
        pl.when(has_down)(lambda: to_down(s, l).start())
        pl.when(has_up)(lambda: to_up(s, l).start())

    def wait_rims(s, l):
        pl.when(has_up)(lambda: to_down(s, l).wait_recv())
        pl.when(has_down)(lambda: to_up(s, l).wait_recv())

    def wait_rims_sent(s, l):
        pl.when(has_down)(lambda: to_down(s, l).wait_send())
        pl.when(has_up)(lambda: to_up(s, l).wait_send())

    def assemble(dst, s, l):
        low = height + HALF_ROWS
        for part in range(2):
            for c in range(tiles):
                lanes = slice(c * LANES, (c + 1) * LANES)
                dst[part, c, 0:HALF_ROWS] = top[s, l, part, :, lanes]
                dst[part, c, HALF_ROWS:2 * HALF_ROWS] = edge[s, l, 0, part, :, lanes]
                dst[part, c, 2 * HALF_ROWS:2 * HALF_ROWS + inner] = mid[s, l, part, :, lanes]
                dst[part, c, height:low] = edge[s, l, 1, part, :, lanes]
                dst[part, c, low:low + HALF_ROWS] = bot[s, l, part, :, lanes]

    def window(fields):
        count = len(fields)
        for f, field in enumerate(fields):
            pbuf[f] = field
        for f in range(count):
            sbuf[f, :, 0:span - 2] = (pbuf[f, :, 0:span - 2] + pbuf[f, :, 1:span - 1]) + pbuf[f, :, 2:span]
        for f in range(count):
            total = (sbuf[f, :, 0:height] + sbuf[f, :, 3:height + 3]) + sbuf[f, :, 6:height + 6]
            high = total.astype(jnp.bfloat16)
            low = (total - high.astype(jnp.float32)).astype(jnp.bfloat16)
            for c in range(tiles):
                lhs[f * height:(f + 1) * height, c * LANES:(c + 1) * LANES] = high[c]
                lhs[(count + f) * height:(count + f + 1) * height, c * LANES:(c + 1) * LANES] = low[c]
        sums = jnp.dot(lhs[0:2 * count * height], band[...], preferred_element_type=jnp.float32)
        return [sums[f * height:(f + 1) * height] + sums[(count + f) * height:(count + f + 1) * height]
                for f in range(count)]

    def local_power():
        fields = []
        for i in range(local):
            real, imag = mine[i, 0], mine[i, 1]
            fields.append(real * real + imag * imag)
        for i, power in enumerate(window(fields)):
            pw[i] = power

    def compute(s, l, oth_real, oth_imag):
        fields = [oth_real * oth_real + oth_imag * oth_imag]
        for i in range(local):
            real, imag = mine[i, 0], mine[i, 1]
            fields.append(real * oth_real + imag * oth_imag)
            fields.append(imag * oth_real - real * oth_imag)
        sums = window(fields)
        date = s * local + l
        for i in range(local):
            factor = lax.rsqrt(pw[i] * sums[0] + epsilon)
            coh[i, date, 0] = sums[1 + 2 * i] * factor
            coh[i, date, 1] = sums[2 + 2 * i] * factor

    load.wait()
    for l in range(local):
        edge[me, l, 0] = own[l, :, 0:HALF_ROWS]
        edge[me, l, 1] = own[l, :, height - HALF_ROWS:height]
        mid[me, l] = own[l, :, HALF_ROWS:height - HALF_ROWS]
    greeters = functools.reduce(jnp.add, [jnp.where(near, 1, 0) for near in (has_left, has_right, has_up, has_down)])
    pl.semaphore_wait(barrier, greeters)

    for k, l in chunks:
        pl.when(has_right)(lambda: to_right(k, me, l).start())
        pl.when(has_left)(lambda: to_left(k, me, l).start())
        if k == 0:
            send_rims(me, l)
    def own_dates():
        for l in range(local):
            wait_rims(me, l)
            assemble(mine.at[l], me, l)
        local_power()
        for l in range(local):
            compute(me, l, mine[l, 0], mine[l, 1])

    def finish(t, l):
        for s, there in ((me - 1 - t, me - 1 - t >= 0), (me + 1 + t, me + 1 + t < n)):
            @pl.when(there)
            def _(s=s):
                wait_rims(s, l)
                assemble(other, s, l)
                compute(s, l, other[0], other[1])

    def step(t, carry):
        s_left, s_right = me - 1 - t, me + 1 + t
        for k, l in chunks:
            @pl.when(s_left >= 0)
            def _():
                to_right(k, s_left, l).wait_recv()
                pl.when(has_right)(lambda: to_right(k, s_left, l).start())
                if k == 0:
                    send_rims(s_left, l)

            @pl.when(s_right < n)
            def _():
                to_left(k, s_right, l).wait_recv()
                pl.when(has_left)(lambda: to_left(k, s_right, l).start())
                if k == 0:
                    send_rims(s_right, l)

            if k == 0 and l == local - 1:
                pl.when(jnp.logical_and(at_end, t == 0))(own_dates)
            if k == 1:
                pl.when(at_end)(lambda: finish(t, l))
        return carry

    if n > 1:
        lax.fori_loop(0, n - 1, step, 0)

        @pl.when(jnp.logical_not(at_end))
        def _():
            own_dates()

            def late(t, carry):
                for l in range(local):
                    finish(t, l)
                return carry

            lax.fori_loop(0, n - 1, late, 0)
    else:
        own_dates()

    for k, l in chunks:
        pl.when(has_right)(lambda: to_right(k, me, l).wait_send())
        pl.when(has_left)(lambda: to_left(k, me, l).wait_send())
        if k == 0:
            wait_rims_sent(me, l)

    def drain(t, carry):
        s_left, s_right = me - 1 - t, me + 1 + t
        for k, l in chunks:
            @pl.when(s_left >= 0)
            def _():
                pl.when(has_right)(lambda: to_right(k, s_left, l).wait_send())
                if k == 0:
                    wait_rims_sent(s_left, l)

            @pl.when(s_right < n)
            def _():
                pl.when(has_left)(lambda: to_left(k, s_right, l).wait_send())
                if k == 0:
                    wait_rims_sent(s_right, l)
        return carry

    if n > 1:
        lax.fori_loop(0, n - 1, drain, 0)


def order_kernel(plan_ref, coh, out, sem):
    dates = out.shape[1]

    def copy(k):
        return pltpu.make_async_copy(coh.at[:, plan_ref[k]], out.at[:, k], sem.at[k])

    def start(k, carry):
        copy(k).start()
        return carry

    def finish(k, carry):
        copy(k).wait()
        return carry

    lax.fori_loop(0, dates, start, 0)
    lax.fori_loop(0, dates, finish, 0)


def body(n, rows_n, stack_data, plan):
    local, _, height, width = stack_data.shape
    dates = local * n
    tiles = width // LANES
    fields = 2 * local + 1
    span = height + 2 * HALF_ROWS
    kind = jax.ShapeDtypeStruct((local, dates, 2, height, width), jnp.float32)
    dma = pltpu.SemaphoreType.DMA
    result_bytes = local * dates * 2 * height * width * 4
    stack_data = pltpu.with_memory_space_constraint(stack_data, pltpu.HBM)
    coh = pl.pallas_call(
        functools.partial(gather_kernel, n, rows_n),
        out_shape=kind,
        in_specs=[pl.BlockSpec(memory_space=pltpu.HBM)],
        out_specs=pl.BlockSpec(memory_space=pltpu.VMEM),
        scratch_shapes=[
            pltpu.VMEM((local, 2, height, width), jnp.float32),
            pltpu.VMEM((n, local, 2, 2, HALF_ROWS, width), jnp.float32),
            pltpu.VMEM((n, local, 2, height - 2 * HALF_ROWS, width), jnp.float32),
            pltpu.VMEM((n, local, 2, HALF_ROWS, width), jnp.float32),
            pltpu.VMEM((n, local, 2, HALF_ROWS, width), jnp.float32),
            pltpu.VMEM((local, 2, tiles, span, LANES), jnp.float32),
            pltpu.VMEM((2, tiles, span, LANES), jnp.float32),
            pltpu.VMEM((width, width), jnp.bfloat16),
            pltpu.VMEM((fields, tiles, span, LANES), jnp.float32),
            pltpu.VMEM((fields, tiles, span, LANES), jnp.float32),
            pltpu.VMEM((2 * fields * height, width), jnp.bfloat16),
            pltpu.VMEM((local, height, width), jnp.float32),
            dma,
            dma((2, n, local)), dma((2, n, local)), dma((2, n, local)),
            dma((n, local)), dma((n, local)), dma((n, local)), dma((n, local)),
        ],
        compiler_params=pltpu.CompilerParams(
            collective_id=0, has_side_effects=True,
            vmem_limit_bytes=4 * result_bytes + (8 << 20)),
    )(stack_data)
    return pl.pallas_call(
        order_kernel,
        out_shape=kind,
        in_specs=[pl.BlockSpec(memory_space=pltpu.SMEM), pl.BlockSpec(memory_space=pltpu.VMEM)],
        out_specs=pl.BlockSpec(memory_space=pl.ANY),
        scratch_shapes=[dma((dates,))],
        compiler_params=pltpu.CompilerParams(vmem_limit_bytes=2 * result_bytes + (2 << 20)),
    )(plan, coh)


def solution(mesh):
    placed = (P(("grp", "date"), None, "row", None), P())
    return jax.shard_map(
        functools.partial(body, mesh.shape["date"], mesh.shape["row"]),
        mesh=mesh,
        in_specs=placed,
        out_specs=P(("grp", "date"), None, None, "row", None),
        check_vma=False,
    )
```

profile of v0, /device:TPU:1, one launch (start us, length us, event | category | flops | bytes accessed | tf_op | source)
XLA Modules:
  0.0 19.0 jit_solution(7746311427511381973)
XLA Ops:
  0.0 0.0 copy-start
  0.0 17.4 %shard_map.28.coh = f32[2,8,2,16,512]{4,3,2,1,0:T(8,128)S(1)} custom-call(f32[2,2,16,512]{3,2,1,0:T(8,128)} %x_ref.1), custom_call_target="tpu_custom_call" | custom-call | tf_op jit(solution)/shard_map/pallas_call | solution.py:259
  17.4 0.0 copy-done
  17.4 1.6 %shard_map.29 = f32[2,8,2,16,512]{4,3,2,1,0:T(8,128)} custom-call(s32[8]{0:T(128)S(1)} %copy-done, f32[2,8,2,16,512]{4,3,2,1,0:T(8,128)S(1)} %shard_map.28.coh), custom_call_target="tpu_custom_call" | custom-call | tf_op jit(solution)/shard_map/pallas_call | solution.py:285
Async XLA Ops:
  0.0 17.4 %copy-start = (s32[8]{0:T(128)S(1)}, s32[8]{0:T(128)}, u32[]{:S(2)}) copy-start(s32[8]{0:T(128)} %plan_ref.1) | copy-start | bytes 100
where the time goes:
time: 19.1 us; the launch traced here: 19 us
  Pallas kernels  19 us (99%)
    pallas_call x1, Pallas kernels, body(): pl.pallas_call(functools.partial(gather_kernel, n, rows_n), out_shape=kin...  17.4 us
    pallas_call x1, Pallas kernels, body(): pl.pallas_call(order_kernel, out_shape=kind, in_specs=[pl.BlockSpec(memor...  1.57 us

commit v1 on v0

v1 whole, which is shorter than its diff:
```python
import functools

import jax
import jax.numpy as jnp
from jax import lax
from jax.experimental import pallas as pl
from jax.experimental.pallas import tpu as pltpu
from jax.sharding import PartitionSpec as P

HALF_ROWS = 4
HALF_COLS = 16
LANES = 128

epsilon = 1e-06


EDGE, MID = 0, 1


def chain_of_four():
    def send(s, k, d):
        return ("send", s, k, d)

    def take(s, k):
        return ("take", s, k)

    own_right = {d: [send(d, EDGE, d + 1), send(d, MID, d + 1)] for d in range(3)}
    enter = [("load",), ("down",), ("right",)]
    spots = {}
    for core in range(2):
        spots[0, core] = [enter, own_right[0]]
        spots[3, core] = [[("load",), ("down",)], []]
    spots[0, 0] += [[take(1, EDGE), take(2, EDGE)], [take(3, EDGE)], []]
    spots[0, 1] += [[take(1, EDGE)], [take(2, EDGE), take(3, EDGE)], []]
    for core in range(2):
        spots[3, core] += [[take(2, EDGE), take(1, EDGE)], [take(0, EDGE)], []]
    spots[3, 0][0] = [send(3, EDGE, 0), send(3, EDGE, 2), send(3, MID, 0), send(3, MID, 2), send(3, EDGE, 1),
                      send(3, MID, 1)] + spots[3, 0][0]
    spots[3, 1][0] = [send(3, EDGE, 2), send(3, MID, 2)] + spots[3, 1][0]
    first = [send(1, EDGE, 0), send(1, MID, 0)] + enter + own_right[1]
    spots[1, 0] = [first, [send(0, EDGE, 2), send(0, MID, 2)], [], [take(2, EDGE), take(3, EDGE)], []]
    spots[1, 1] = [first, [send(2, EDGE, 0), send(0, EDGE, 2), send(3, EDGE, 0), send(0, MID, 2), send(2, MID, 0),
                           send(3, MID, 0)], [], [], []]
    onward = [send(1, EDGE, 3), send(0, EDGE, 3), send(1, MID, 3), send(0, MID, 3)]
    spots[2, 0] = [[send(2, EDGE, 0), send(2, EDGE, 1), send(2, MID, 0)] + enter + own_right[2],
                   onward + [take(3, EDGE), send(2, MID, 1)], [], [], []]
    spots[2, 1] = [[send(2, EDGE, 1), send(2, MID, 1)] + enter + own_right[2],
                   [send(3, EDGE, 1), onward[0], send(3, MID, 1)] + onward[1:], [], [], []]
    return spots, {0: (1, 2, 3), 1: (0, 2, 3), 2: (1, 0, 3), 3: (2, 1, 0)}


def gather_kernel(n, rows_n, x_ref, coh, buf, top, bot, mine, other, band, pbuf, sbuf, lhs, pw,
                  load_sem, ready, recv, sent, rim_recv, rim_sent):
    local, _, height, width = x_ref.shape
    tiles = width // LANES
    span = height + 2 * HALF_ROWS
    me = lax.axis_index("date")
    row = lax.axis_index("row")
    has_left, has_right = me > 0, me < n - 1
    has_up, has_down = row > 0, row < rows_n - 1

    def count(*flags):
        return functools.reduce(jnp.add, [jnp.where(flag, 1, 0) for flag in flags])

    def tell(sem, axis, index):
        pl.semaphore_signal(sem, inc=1, device_id={axis: index}, device_id_type=pl.DeviceIdType.MESH)

    barrier = pltpu.get_barrier_semaphore()
    pl.when(has_down)(lambda: tell(barrier, "row", row + 1))
    load = pltpu.make_async_copy(x_ref, buf.at[pl.ds(me * local, local)], load_sem)
    load.start()
    pl.when(jnp.logical_or(has_left, has_up))(lambda: pl.semaphore_wait(barrier, count(has_left, has_up)))
    pl.when(has_right)(lambda: tell(barrier, "date", me + 1))
    pl.when(has_left)(lambda: tell(ready.at[0], "date", me - 1))
    pl.when(has_up)(lambda: tell(ready.at[1], "row", row - 1))

    def remote(src, dst, send_sem, recv_sem, axis, index):
        return pltpu.make_async_remote_copy(
            src_ref=src, dst_ref=dst, send_sem=send_sem, recv_sem=recv_sem,
            device_id={axis: index}, device_id_type=pl.DeviceIdType.MESH)

    upper, lower = slice(0, HALF_ROWS), slice(height - HALF_ROWS, height)
    middle = slice(HALF_ROWS, height - HALF_ROWS)

    def send(source, s, k, l, d, side):
        for rows in ((upper, lower), (middle,))[k]:
            remote(source.at[l, :, rows], buf.at[s * local + l, :, rows], sent.at[side], recv.at[s, k, l],
                   "date", d).start()

    def arrived(s, k, l):
        ref = buf.at[s * local + l, :, middle if k else slice(0, 2 * HALF_ROWS)]
        remote(ref, ref, sent.at[0], recv.at[s, k, l], "date", me).wait_recv()

    def all_sent(side, dates):
        ref = buf.at[pl.ds(0, dates)]
        remote(ref, ref, sent.at[side], sent.at[side], "date", me).wait_send()

    def rim_down(s, l):
        return remote(buf.at[s * local + l, :, lower], top.at[s, l], rim_sent.at[0], rim_recv.at[0, s, l], "row", row + 1)

    def rim_up(s, l):
        return remote(buf.at[s * local + l, :, upper], bot.at[s, l], rim_sent.at[1], rim_recv.at[1, s, l], "row", row - 1)

    def send_rims(s, l):
        pl.when(has_down)(lambda: rim_down(s, l).start())
        pl.when(has_up)(lambda: rim_up(s, l).start())

    def wait_rims(s, l):
        pl.when(has_up)(lambda: rim_down(s, l).wait_recv())
        pl.when(has_down)(lambda: rim_up(s, l).wait_recv())

    def prepare():
        @pl.when(row == 0)
        def _():
            top[...] = jnp.zeros_like(top)

        @pl.when(row == rows_n - 1)
        def _():
            bot[...] = jnp.zeros_like(bot)

        col_in = lax.broadcasted_iota(jnp.int32, (width, width), 0)
        col_out = lax.broadcasted_iota(jnp.int32, (width, width), 1)
        band[...] = jnp.where(jnp.abs(col_in - col_out) <= HALF_COLS, 1.0, 0.0).astype(jnp.bfloat16)

    def assemble(dst, s, l):
        low = height + HALF_ROWS
        for part in range(2):
            for c in range(tiles):
                lanes = slice(c * LANES, (c + 1) * LANES)
                dst[part, c, 0:HALF_ROWS] = top[s, l, part, :, lanes]
                dst[part, c, HALF_ROWS:low] = buf[s * local + l, part, :, lanes]
                dst[part, c, low:low + HALF_ROWS] = bot[s, l, part, :, lanes]

    def window(fields):
        count = len(fields)
        for f, field in enumerate(fields):
            pbuf[f] = field
        for f in range(count):
            sbuf[f, :, 0:span - 2] = (pbuf[f, :, 0:span - 2] + pbuf[f, :, 1:span - 1]) + pbuf[f, :, 2:span]
        for f in range(count):
            total = (sbuf[f, :, 0:height] + sbuf[f, :, 3:height + 3]) + sbuf[f, :, 6:height + 6]
            high = total.astype(jnp.bfloat16)
            low = (total - high.astype(jnp.float32)).astype(jnp.bfloat16)
            for c in range(tiles):
                lhs[f * height:(f + 1) * height, c * LANES:(c + 1) * LANES] = high[c]
                lhs[(count + f) * height:(count + f + 1) * height, c * LANES:(c + 1) * LANES] = low[c]
        sums = jnp.dot(lhs[0:2 * count * height], band[...], preferred_element_type=jnp.float32)
        return [sums[f * height:(f + 1) * height] + sums[(count + f) * height:(count + f + 1) * height]
                for f in range(count)]

    def local_power():
        fields = []
        for i in range(local):
            real, imag = mine[i, 0], mine[i, 1]
            fields.append(real * real + imag * imag)
        for i, power in enumerate(window(fields)):
            pw[i] = power

    def compute(s, l, oth):
        oth_real, oth_imag = oth[0], oth[1]
        fields = [oth_real * oth_real + oth_imag * oth_imag]
        for i in range(local):
            real, imag = mine[i, 0], mine[i, 1]
            fields.append(real * oth_real + imag * oth_imag)
            fields.append(imag * oth_real - real * oth_imag)
        sums = window(fields)
        date = s * local + l
        for i in range(local):
            factor = lax.rsqrt(pw[i] * sums[0] + epsilon)
            coh[i, date, 0] = sums[1 + 2 * i] * factor
            coh[i, date, 1] = sums[2 + 2 * i] * factor

    def own_dates():
        for l in range(local):
            wait_rims(me, l)
            assemble(mine.at[l], me, l)
        local_power()
        for l in range(local):
            compute(me, l, mine.at[l])

    def finish(s, l):
        wait_rims(s, l)
        assemble(other, s, l)
        compute(s, l, other)

    schedule, partners = chain_of_four() if n == 4 else ({}, {})
    held = {spot: [] for spot in schedule}
    pieces = {spot: [0, 0] for spot in schedule}

    def at(spot):
        return jnp.logical_and(me == spot[0], lax.rem(row, 2) == spot[1])

    def take(spot, s, k, l):
        if s != spot[0] and (s, k, l) not in held[spot]:
            held[spot].append((s, k, l))
            arrived(s, k, l)
            if k == EDGE:
                send_rims(s, l)

    def perform(spot, ops):
        here = spot[0]
        for op, *rest in ops:
            if op == "send":
                s, k, d = rest
                for l in range(local):
                    take(spot, s, k, l)
                    source = x_ref if s == here and d < here else buf.at[pl.ds(s * local, local)]
                    pieces[spot][d > here] += 1
                    send(source, s, k, l, d, int(d > here))
            elif op == "take":
                for l in range(local):
                    take(spot, rest[0], rest[1], l)
            elif op == "load":
                load.wait()
                for l in range(local):
                    pl.when(has_up)(lambda: rim_up(here, l).start())
            elif op == "down":
                @pl.when(has_down)
                def _():
                    pl.semaphore_wait(ready.at[1], 1)
                    for l in range(local):
                        rim_down(here, l).start()
            elif op == "right" and here < n - 1:
                pl.semaphore_wait(ready.at[0], 1)

    def everywhere(step):
        for spot in schedule:
            pl.when(at(spot))(functools.partial(step, spot))

    def short_chain():
        everywhere(lambda spot: perform(spot, schedule[spot][0]))
        prepare()
        everywhere(lambda spot: perform(spot, schedule[spot][1]))
        own_dates()
        for t in range(n - 1):
            everywhere(lambda spot: perform(spot, schedule[spot][2 + t]))
            s = functools.reduce(jnp.add, [jnp.where(me == d, partners[d][t], 0) for d in partners])
            for l in range(local):
                def rest(spot):
                    for k in (EDGE, MID):
                        for m in range(local) if k == EDGE else (l,):
                            take(spot, partners[spot[0]][t], k, m)

                everywhere(rest)
                finish(s, l)

        def drain(spot):
            for side in range(2):
                if pieces[spot][side]:
                    all_sent(side, pieces[spot][side] // 2)

        everywhere(drain)

    def long_chain():
        mine_now = buf.at[pl.ds(me * local, local)]
        chunks = [(k, l) for k in (EDGE, MID) for l in range(local)]

        @pl.when(has_left)
        def _():
            for k, l in chunks:
                send(x_ref, me, k, l, me - 1, me)

        load.wait()
        for l in range(local):
            pl.when(has_up)(lambda: rim_up(me, l).start())

        @pl.when(has_right)
        def _():
            pl.semaphore_wait(ready.at[0], 1)
            for k, l in chunks:
                send(mine_now, me, k, l, me + 1, n)

        @pl.when(has_down)
        def _():
            pl.semaphore_wait(ready.at[1], 1)
            for l in range(local):
                rim_down(me, l).start()

        prepare()

        def step(t, carry):
            s_left, s_right = me - 1 - t, me + 1 + t
            for k, l in chunks:
                for s, there, onward, to in ((s_right, s_right < n, has_left, me - 1), (s_left, s_left >= 0, has_right, me + 1)):
                    @pl.when(there)
                    def _():
                        arrived(s, k, l)
                        pl.when(onward)(lambda: send(buf.at[pl.ds(s * local, local)], s, k, l, to, s))
                        if k == EDGE:
                            send_rims(s, l)
            return carry

        lax.fori_loop(0, n - 1, step, 0)
        own_dates()

        def late(s, carry):
            @pl.when(s != me)
            def _():
                for l in range(local):
                    finish(s, l)
            return carry

        lax.fori_loop(0, n, late, 0)
        pl.when(has_left)(lambda: all_sent(me, local))
        pl.when(has_right)(lambda: all_sent(n, local))

        def drain(s, carry):
            passed = jnp.logical_or(jnp.logical_and(s > me, has_left), jnp.logical_and(s < me, has_right))
            pl.when(passed)(lambda: all_sent(s, local))
            return carry

        lax.fori_loop(0, n, drain, 0)

    if schedule:
        short_chain()
    else:
        long_chain()
    pl.when(has_down)(lambda: remote(top, top, rim_sent.at[0], rim_sent.at[0], "row", row).wait_send())
    pl.when(has_up)(lambda: remote(bot, bot, rim_sent.at[1], rim_sent.at[1], "row", row).wait_send())


def order_kernel(plan_ref, coh, out, sem):
    dates = out.shape[1]
    plan = plan_ref[...].reshape(1, dates)
    place = lax.broadcasted_iota(jnp.int32, (1, dates), 1)

    def copy(k):
        return pltpu.make_async_copy(coh.at[:, jnp.sum(jnp.where(place == k, plan, 0))], out.at[:, k], sem)

    def start(k, carry):
        copy(k).start()
        return carry

    if dates <= 8:
        for k in range(dates):
            start(k, 0)
    else:
        lax.fori_loop(0, dates, start, 0)
    pltpu.make_async_copy(coh, out, sem).wait()


def body(n, rows_n, stack_data, plan):
    local, _, height, width = stack_data.shape
    dates = local * n
    tiles = width // LANES
    fields = 2 * local + 1
    span = height + 2 * HALF_ROWS
    kind = jax.ShapeDtypeStruct((local, dates, 2, height, width), jnp.float32)
    dma = pltpu.SemaphoreType.DMA
    result_bytes = local * dates * 2 * height * width * 4
    stack_data = pltpu.with_memory_space_constraint(stack_data, pltpu.HBM)
    coh = pl.pallas_call(
        functools.partial(gather_kernel, n, rows_n),
        out_shape=kind,
        in_specs=[pl.BlockSpec(memory_space=pltpu.HBM)],
        out_specs=pl.BlockSpec(memory_space=pltpu.VMEM),
        scratch_shapes=[
            pltpu.VMEM((n * local, 2, height, width), jnp.float32),
            pltpu.VMEM((n, local, 2, HALF_ROWS, width), jnp.float32),
            pltpu.VMEM((n, local, 2, HALF_ROWS, width), jnp.float32),
            pltpu.VMEM((local, 2, tiles, span, LANES), jnp.float32),
            pltpu.VMEM((2, tiles, span, LANES), jnp.float32),
            pltpu.VMEM((width, width), jnp.bfloat16),
            pltpu.VMEM((fields, tiles, span, LANES), jnp.float32),
            pltpu.VMEM((fields, tiles, span, LANES), jnp.float32),
            pltpu.VMEM((2 * fields * height, width), jnp.bfloat16),
            pltpu.VMEM((local, height, width), jnp.float32),
            dma, pltpu.SemaphoreType.REGULAR((2,)),
            dma((n, 2, local)), dma((2,) if n == 4 else (n + 1,)), dma((2, n, local)), dma((2,)),
        ],
        compiler_params=pltpu.CompilerParams(
            collective_id=0, has_side_effects=True,
            vmem_limit_bytes=4 * result_bytes + (8 << 20)),
    )(stack_data)
    return pl.pallas_call(
        order_kernel,
        out_shape=kind,
        in_specs=[pl.BlockSpec(memory_space=pltpu.VMEM), pl.BlockSpec(memory_space=pltpu.VMEM)],
        out_specs=pl.BlockSpec(memory_space=pl.ANY),
        scratch_shapes=[dma],
        compiler_params=pltpu.CompilerParams(vmem_limit_bytes=2 * result_bytes + (2 << 20)),
    )(plan, coh)


def solution(mesh):
    placed = (P(("grp", "date"), None, "row", None), P())
    return jax.shard_map(
        functools.partial(body, mesh.shape["date"], mesh.shape["row"]),
        mesh=mesh,
        in_specs=placed,
        out_specs=P(("grp", "date"), None, None, "row", None),
        check_vma=False,
    )
```

time: 19.1 us -> 16.4 us (0.86)
  Pallas kernels: 19 us -> 16.2 us
    pallas_call x1, Pallas kernels: 17.4 us -> 15.1 us  [body(): pl.pallas_call(functools.partial(gather_kernel, n, rows_n), out_shape=kin...]
    pallas_call x1, Pallas kernels: 1.57 us -> 1.09 us  [body(): pl.pallas_call(order_kernel, out_shape=kind, in_specs=[pl.BlockSpec(memor...]
where the time goes in v1:
time: 16.4 us; the launch traced here: 16.3 us
  Pallas kernels  16.2 us (99%)
    pallas_call x1, Pallas kernels, body(): pl.pallas_call(functools.partial(gather_kernel, n, rows_n), out_shape=kin...  15.1 us
    pallas_call x1, Pallas kernels, body(): pl.pallas_call(order_kernel, out_shape=kind, in_specs=[pl.BlockSpec(memor...  1.09 us

profile of v1, /device:TPU:1, one launch (start us, length us, event | category | flops | bytes accessed | tf_op | source)
XLA Modules:
  0.0 16.3 jit_solution(16867767777100640404)
XLA Ops:
  0.0 0.0 copy-start
  0.0 15.1 %shard_map.28.coh = f32[2,8,2,16,512]{4,3,2,1,0:T(8,128)S(1)} custom-call(f32[2,2,16,512]{3,2,1,0:T(8,128)} %x_ref.1), custom_call_target="tpu_custom_call" | custom-call | tf_op jit(solution)/shard_map/pallas_call | solution.py:352
  15.2 0.0 copy-done
  15.2 1.1 %shard_map.29 = f32[2,8,2,16,512]{4,3,2,1,0:T(8,128)} custom-call(s32[8]{0:T(128)S(1)} %copy-done, f32[2,8,2,16,512]{4,3,2,1,0:T(8,128)S(1)} %shard_map.28.coh), custom_call_target="tpu_custom_call" | custom-call | tf_op jit(solution)/shard_map/pallas_call | solution.py:375
Async XLA Ops:
  0.0 15.2 %copy-start = (s32[8]{0:T(128)S(1)}, s32[8]{0:T(128)}, u32[]{:S(2)}) copy-start(s32[8]{0:T(128)} %plan_ref.1) | copy-start | bytes 100

commit v2 on v1

v2 whole, which is shorter than its diff:
```python
import functools

import jax
import jax.numpy as jnp
from jax import lax
from jax.experimental import pallas as pl
from jax.experimental.pallas import tpu as pltpu
from jax.sharding import PartitionSpec as P

HALF_ROWS = 4
HALF_COLS = 16
LANES = 128

epsilon = 1e-06

EDGE, MID = 0, 1


def chain_of_four():
    def send(s, k, d):
        return ("send", s, k, d)

    def take(s, k):
        return ("take", s, k)

    def right(d):
        return [("load",), ("down",), ("right",), send(d, EDGE, d + 1), send(d, MID, d + 1)]

    places = {}
    begin = right(0)
    places[0, 0] = [begin, [], [take(1, EDGE), take(2, EDGE)], [take(3, EDGE)], []]
    places[0, 1] = [begin, [], [take(1, EDGE)], [take(2, EDGE), take(3, EDGE)], []]
    begin = [send(1, EDGE, 0), send(1, MID, 0)] + right(1)
    places[1, 0] = [begin, [send(0, EDGE, 2), send(0, MID, 2)], [], [take(2, EDGE), take(3, EDGE)], []]
    places[1, 1] = [begin, [send(2, EDGE, 0), send(0, EDGE, 2), send(2, MID, 0), send(3, EDGE, 0), send(0, MID, 2),
                            send(3, MID, 0)], [], [], []]
    places[2, 0] = [[send(2, EDGE, 0), send(2, EDGE, 1), send(2, MID, 0)] + right(2),
                    [send(1, EDGE, 3), send(0, EDGE, 3), send(1, MID, 3), send(2, MID, 1), send(0, MID, 3),
                     take(3, EDGE)], [], [], []]
    places[2, 1] = [[send(2, EDGE, 1), send(2, MID, 1)] + right(2),
                    [send(3, EDGE, 1), send(1, EDGE, 3), send(3, MID, 1), send(0, EDGE, 3), send(1, MID, 3),
                     send(0, MID, 3)], [], [], []]
    places[3, 0] = [[send(3, EDGE, 0), send(3, EDGE, 2), send(3, MID, 0), send(3, MID, 2), send(3, EDGE, 1),
                     ("load",), ("down",)], [], [take(2, EDGE), take(1, EDGE), send(3, MID, 1)], [take(0, EDGE)], []]
    places[3, 1] = [[send(3, EDGE, 2), send(3, MID, 2), ("load",), ("down",)], [], [take(2, EDGE), take(1, EDGE)],
                    [take(0, EDGE)], []]
    return places, {0: (1, 2, 3), 1: (0, 2, 3), 2: (1, 0, 3), 3: (2, 1, 0)}


def pick(me, values):
    return functools.reduce(jnp.add, [jnp.where(me == d, value, 0) for d, value in values.items()])


def window(fields, band, pbuf, sbuf, lhs):
    count = len(fields)
    _, tiles, span, _ = pbuf.shape
    height = span - 2 * HALF_ROWS
    for f, field in enumerate(fields):
        pbuf[f] = field
    for f in range(count):
        sbuf[f, :, 0:span - 2] = (pbuf[f, :, 0:span - 2] + pbuf[f, :, 1:span - 1]) + pbuf[f, :, 2:span]
    for f in range(count):
        total = (sbuf[f, :, 0:height] + sbuf[f, :, 3:height + 3]) + sbuf[f, :, 6:height + 6]
        high = total.astype(jnp.bfloat16)
        low = (total - high.astype(jnp.float32)).astype(jnp.bfloat16)
        for c in range(tiles):
            lhs[f * height:(f + 1) * height, c * LANES:(c + 1) * LANES] = high[c]
            lhs[(count + f) * height:(count + f + 1) * height, c * LANES:(c + 1) * LANES] = low[c]
    sums = jnp.dot(lhs[0:2 * count * height], band[...], preferred_element_type=jnp.float32)
    return [sums[f * height:(f + 1) * height] + sums[(count + f) * height:(count + f + 1) * height]
            for f in range(count)]


def partner_results(mine, other, pw, dates, put, band, *work):
    local = mine.shape[0]
    fields = []
    for l in dates:
        real, imag = other[l, 0], other[l, 1]
        fields.append(real * real + imag * imag)
        for i in range(local):
            own_real, own_imag = mine[i, 0], mine[i, 1]
            fields.append(own_real * real + own_imag * imag)
            fields.append(own_imag * real - own_real * imag)
    sums = iter(window(fields, band, *work))
    for l in dates:
        power = next(sums)
        for i in range(local):
            factor = lax.rsqrt(pw[i] * power + epsilon)
            put(i, l, next(sums) * factor, next(sums) * factor)


def gather_kernel(n, rows_n, x_ref, coh, mine, other, pw, band, buf, top, bot, pbuf, sbuf, lhs,
                  load_sem, ready, recv, sent, rim_recv, rim_sent):
    local, _, height, width = x_ref.shape
    tiles = width // LANES
    me = lax.axis_index("date")
    row = lax.axis_index("row")
    has_left, has_right = me > 0, me < n - 1
    at_end = jnp.logical_not(jnp.logical_and(has_left, has_right))
    has_up, has_down = row > 0, row < rows_n - 1

    def count(*flags):
        return functools.reduce(jnp.add, [jnp.where(flag, 1, 0) for flag in flags])

    def tell(sem, axis, index):
        pl.semaphore_signal(sem, inc=1, device_id={axis: index}, device_id_type=pl.DeviceIdType.MESH)

    barrier = pltpu.get_barrier_semaphore()
    pl.when(has_down)(lambda: tell(barrier, "row", row + 1))
    load = pltpu.make_async_copy(x_ref, buf.at[pl.ds(me * local, local)], load_sem)
    load.start()
    pl.when(jnp.logical_or(has_left, has_up))(lambda: pl.semaphore_wait(barrier, count(has_left, has_up)))
    pl.when(has_right)(lambda: tell(barrier, "date", me + 1))
    pl.when(has_left)(lambda: tell(ready.at[0], "date", me - 1))
    pl.when(has_up)(lambda: tell(ready.at[1], "row", row - 1))

    def remote(src, dst, send_sem, recv_sem, axis, index):
        return pltpu.make_async_remote_copy(
            src_ref=src, dst_ref=dst, send_sem=send_sem, recv_sem=recv_sem,
            device_id={axis: index}, device_id_type=pl.DeviceIdType.MESH)

    upper, lower = slice(0, HALF_ROWS), slice(height - HALF_ROWS, height)
    middle = slice(HALF_ROWS, height - HALF_ROWS)
    both = slice(0, 2)
    pieces = {EDGE: (0,), MID: (1, 2)}
    areas = [[(both, upper), (both, lower)], [(slice(0, 1), middle)], [(slice(1, 2), middle)]]

    def send(source, s, p, l, d, sem):
        for part, rows in areas[p]:
            remote(source.at[l, part, rows], buf.at[s * local + l, part, rows], sent.at[sem], recv.at[s, p, l],
                   "date", d).start()

    def arrived(s, p, l):
        part, rows = areas[p][0] if p else (both, slice(0, 2 * HALF_ROWS))
        ref = buf.at[s * local + l, part, rows]
        remote(ref, ref, sent.at[0], recv.at[s, p, l], "date", me).wait_recv()

    def all_sent(sem, dates):
        ref = buf.at[pl.ds(0, dates)]
        remote(ref, ref, sent.at[sem], sent.at[sem], "date", me).wait_send()

    def dates_of(s):
        return buf.at[pl.ds(s * local, local)]

    def rim_down(s, l):
        return remote(buf.at[s * local + l, :, lower], top.at[s, l], rim_sent.at[0], rim_recv.at[0, s, l], "row", row + 1)

    def rim_up(s, l):
        return remote(buf.at[s * local + l, :, upper], bot.at[s, l], rim_sent.at[1], rim_recv.at[1, s, l], "row", row - 1)

    def send_rims(s, l):
        pl.when(has_down)(lambda: rim_down(s, l).start())
        pl.when(has_up)(lambda: rim_up(s, l).start())

    def own_rims_up():
        for l in range(local):
            pl.when(has_up)(lambda: rim_up(me, l).start())

    def own_rims_down():
        @pl.when(has_down)
        def _():
            pl.semaphore_wait(ready.at[1], 1)
            for l in range(local):
                rim_down(me, l).start()

    def prepare():
        @pl.when(row == 0)
        def _():
            top[...] = jnp.zeros_like(top)

        @pl.when(row == rows_n - 1)
        def _():
            bot[...] = jnp.zeros_like(bot)

        col_in = lax.broadcasted_iota(jnp.int32, (width, width), 0)
        col_out = lax.broadcasted_iota(jnp.int32, (width, width), 1)
        band[...] = jnp.where(jnp.abs(col_in - col_out) <= HALF_COLS, 1.0, 0.0).astype(jnp.bfloat16)

    def assemble(dst, s, l):
        pl.when(has_up)(lambda: rim_down(s, l).wait_recv())
        pl.when(has_down)(lambda: rim_up(s, l).wait_recv())
        low = height + HALF_ROWS
        for part in range(2):
            for c in range(tiles):
                lanes = slice(c * LANES, (c + 1) * LANES)
                dst[part, c, 0:HALF_ROWS] = top[s, l, part, :, lanes]
                dst[part, c, HALF_ROWS:low] = buf[s * local + l, part, :, lanes]
                dst[part, c, low:low + HALF_ROWS] = bot[s, l, part, :, lanes]

    def own_dates():
        for l in range(local):
            assemble(mine.at[l], me, l)
        pairs = [(i, j) for i in range(local) for j in range(i + 1, local)]
        fields = [mine[i, 0] * mine[i, 0] + mine[i, 1] * mine[i, 1] for i in range(local)]
        for i, j in pairs:
            fields.append(mine[i, 0] * mine[j, 0] + mine[i, 1] * mine[j, 1])
            fields.append(mine[i, 1] * mine[j, 0] - mine[i, 0] * mine[j, 1])
        sums = window(fields, band, pbuf, sbuf, lhs)

        def put(i, j, real, imag):
            factor = lax.rsqrt(sums[i] * sums[j] + epsilon)
            coh[i, me * local + j, 0] = real * factor
            coh[i, me * local + j, 1] = imag * factor

        for i in range(local):
            pw[i] = sums[i]
            put(i, i, sums[i], jnp.zeros_like(sums[i]))
        for f, (i, j) in enumerate(pairs):
            real, imag = sums[local + 2 * f], sums[local + 2 * f + 1]
            put(i, j, real, imag)
            put(j, i, real, -imag)

    def results(s, dates):
        for l in dates:
            assemble(other.at[l], s, l)

        def put(i, l, real, imag):
            coh[i, s * local + l, 0] = real
            coh[i, s * local + l, 1] = imag

        partner_results(mine, other, pw, dates, put, band, pbuf, sbuf, lhs)

    def short_chain():
        schedule, partners = chain_of_four()
        held = {place: set() for place in schedule}
        shares = {place: [0, 0] for place in schedule}

        def everywhere(step, *dates):
            for place in schedule:
                if place[0] in dates or not dates:
                    here = jnp.logical_and(me == place[0], lax.rem(row, 2) == place[1])
                    pl.when(here)(functools.partial(step, place))

        def take(place, s, k, l):
            for p in pieces[k]:
                if s != place[0] and (s, p, l) not in held[place]:
                    held[place].add((s, p, l))
                    arrived(s, p, l)
                    if k == EDGE:
                        send_rims(s, l)

        def perform(step, place):
            for op, *rest in schedule[place][step]:
                if op == "send":
                    s, k, d = rest
                    for l in range(local):
                        take(place, s, k, l)
                        for p in pieces[k]:
                            send(x_ref if s == place[0] and d < s else dates_of(s), s, p, l, d, int(d > place[0]))
                        shares[place][d > place[0]] += 1
                elif op == "take":
                    for l in range(local):
                        take(place, *rest, l)
                elif op == "load":
                    load.wait()
                    own_rims_up()
                elif op == "down":
                    own_rims_down()
                elif op == "right":
                    pl.semaphore_wait(ready.at[0], 1)

        everywhere(functools.partial(perform, 0))
        prepare()
        everywhere(functools.partial(perform, 1))
        own_dates()
        for t in range(n - 1):
            everywhere(functools.partial(perform, 2 + t))
            s = pick(me, {d: order[t] for d, order in partners.items()})

            def rest(ks, dates, place):
                for k in ks:
                    for l in dates:
                        take(place, partners[place[0]][t], k, l)

            @pl.when(at_end)
            def _():
                everywhere(functools.partial(rest, (EDGE,), range(local)), 0, n - 1)
                for l in range(local):
                    everywhere(functools.partial(rest, (MID,), (l,)), 0, n - 1)
                    results(s, (l,))

            @pl.when(jnp.logical_not(at_end))
            def _():
                everywhere(functools.partial(rest, (EDGE, MID), range(local)), *range(1, n - 1))
                results(s, tuple(range(local)))

        def drain(place):
            for side, share in enumerate(shares[place]):
                if share:
                    all_sent(side, share // 2)

        everywhere(drain)

    def long_chain():
        parts = [(p, l) for k in (EDGE, MID) for p in pieces[k] for l in range(local)]

        @pl.when(has_left)
        def _():
            for p, l in parts:
                send(x_ref, me, p, l, me - 1, me)

        load.wait()
        own_rims_up()

        @pl.when(has_right)
        def _():
            pl.semaphore_wait(ready.at[0], 1)
            for p, l in parts:
                send(dates_of(me), me, p, l, me + 1, n)

        own_rims_down()
        prepare()

        def relay(s, onward, to):
            for p, l in parts:
                arrived(s, p, l)
                pl.when(onward)(lambda: send(dates_of(s), s, p, l, to, s))
                if p == 0:
                    send_rims(s, l)

        def step(t, carry):
            s_left, s_right = me - 1 - t, me + 1 + t
            pl.when(s_right < n)(lambda: relay(s_right, has_left, me - 1))
            pl.when(s_left >= 0)(lambda: relay(s_left, has_right, me + 1))
            return carry

        lax.fori_loop(0, n - 1, step, 0)
        own_dates()

        def late(s, carry):
            @pl.when(s != me)
            def _():
                for l in range(local):
                    results(s, (l,))
            return carry

        lax.fori_loop(0, n, late, 0)
        pl.when(has_left)(lambda: all_sent(me, local))
        pl.when(has_right)(lambda: all_sent(n, local))

        def drain(s, carry):
            passed = jnp.logical_or(jnp.logical_and(s > me, has_left), jnp.logical_and(s < me, has_right))
            pl.when(passed)(lambda: all_sent(s, local))
            return carry

        lax.fori_loop(0, n, drain, 0)

    if n == 4:
        short_chain()
    else:
        long_chain()
    pl.when(has_down)(lambda: remote(top, top, rim_sent.at[0], rim_sent.at[0], "row", row).wait_send())
    pl.when(has_up)(lambda: remote(bot, bot, rim_sent.at[1], rim_sent.at[1], "row", row).wait_send())


def order_kernel(plan_ref, coh, out, sem):
    dates = out.shape[1]
    plan = plan_ref[...].reshape(1, dates)
    place = lax.broadcasted_iota(jnp.int32, (1, dates), 1)

    def start(k, carry):
        date = jnp.sum(jnp.where(place == k, plan, 0))
        pltpu.make_async_copy(coh.at[:, date], out.at[:, k], sem).start()
        return carry

    if dates <= 8:
        for k in range(dates):
            start(k, 0)
    else:
        lax.fori_loop(0, dates, start, 0)
    pltpu.make_async_copy(coh, out, sem).wait()


def body(n, rows_n, stack_data, plan):
    local, _, height, width = stack_data.shape
    dates = local * n
    tiles = width // LANES
    fields = (2 * local + 1) * local
    span = height + 2 * HALF_ROWS
    kind = jax.ShapeDtypeStruct((local, dates, 2, height, width), jnp.float32)
    dma = pltpu.SemaphoreType.DMA
    result_bytes = local * dates * 2 * height * width * 4
    stack_data = pltpu.with_memory_space_constraint(stack_data, pltpu.HBM)
    vmem = pl.BlockSpec(memory_space=pltpu.VMEM)
    coh = pl.pallas_call(
        functools.partial(gather_kernel, n, rows_n),
        out_shape=kind,
        in_specs=[pl.BlockSpec(memory_space=pltpu.HBM)],
        out_specs=vmem,
        scratch_shapes=[
            pltpu.VMEM((local, 2, tiles, span, LANES), jnp.float32),
            pltpu.VMEM((local, 2, tiles, span, LANES), jnp.float32),
            pltpu.VMEM((local, height, width), jnp.float32),
            pltpu.VMEM((width, width), jnp.bfloat16),
            pltpu.VMEM((n * local, 2, height, width), jnp.float32),
            pltpu.VMEM((n, local, 2, HALF_ROWS, width), jnp.float32),
            pltpu.VMEM((n, local, 2, HALF_ROWS, width), jnp.float32),
            pltpu.VMEM((fields, tiles, span, LANES), jnp.float32),
            pltpu.VMEM((fields, tiles, span, LANES), jnp.float32),
            pltpu.VMEM((2 * fields * height, width), jnp.bfloat16),
            dma, pltpu.SemaphoreType.REGULAR((2,)),
            dma((n, 3, local)), dma((2,) if n == 4 else (n + 1,)), dma((2, n, local)), dma((2,)),
        ],
        compiler_params=pltpu.CompilerParams(
            collective_id=0, has_side_effects=True,
            vmem_limit_bytes=4 * result_bytes + (8 << 20)),
    )(stack_data)
    return pl.pallas_call(
        order_kernel,
        out_shape=kind,
        in_specs=[vmem, vmem],
        out_specs=pl.BlockSpec(memory_space=pl.ANY),
        scratch_shapes=[dma],
        compiler_params=pltpu.CompilerParams(vmem_limit_bytes=2 * result_bytes + (2 << 20)),
    )(plan, coh)


def solution(mesh):
    placed = (P(("grp", "date"), None, "row", None), P())
    return jax.shard_map(
        functools.partial(body, mesh.shape["date"], mesh.shape["row"]),
        mesh=mesh,
        in_specs=placed,
        out_specs=P(("grp", "date"), None, None, "row", None),
        check_vma=False,
    )
```

time: 16.4 us -> 15.8 us (0.963)
  Pallas kernels: 16.2 us -> 15.6 us
    pallas_call x1, Pallas kernels: 15.1 us -> 14.5 us  [body(): pl.pallas_call(functools.partial(gather_kernel, n, rows_n), out_shape=kin...]
where the time goes in v2:
time: 15.8 us; the launch traced here: 15.6 us
  Pallas kernels  15.6 us (99%)
    pallas_call x1, Pallas kernels, body(): pl.pallas_call(functools.partial(gather_kernel, n, rows_n), out_shape=kin...  14.5 us
    pallas_call x1, Pallas kernels, body(): pl.pallas_call(order_kernel, out_shape=kind, in_specs=[vmem, vmem], out_s...  1.09 us

profile of v2, /device:TPU:1, one launch (start us, length us, event | category | flops | bytes accessed | tf_op | source)
XLA Modules:
  0.0 15.6 jit_solution(5212442591628246361)
XLA Ops:
  0.0 0.0 copy-start
  0.0 14.5 %shard_map.28.coh = f32[2,8,2,16,512]{4,3,2,1,0:T(8,128)S(1)} custom-call(f32[2,2,16,512]{3,2,1,0:T(8,128)} %x_ref.1), custom_call_target="tpu_custom_call" | custom-call | tf_op jit(solution)/shard_map/pallas_call | solution.py:385
  14.5 0.0 copy-done
  14.5 1.1 %shard_map.29 = f32[2,8,2,16,512]{4,3,2,1,0:T(8,128)} custom-call(s32[8]{0:T(128)S(1)} %copy-done, f32[2,8,2,16,512]{4,3,2,1,0:T(8,128)S(1)} %shard_map.28.coh), custom_call_target="tpu_custom_call" | custom-call | tf_op jit(solution)/shard_map/pallas_call | solution.py:408
Async XLA Ops:
  0.0 14.5 %copy-start = (s32[8]{0:T(128)S(1)}, s32[8]{0:T(128)}, u32[]{:S(2)}) copy-start(s32[8]{0:T(128)} %plan_ref.1) | copy-start | bytes 100

commit v3 on v2

--- a/solution.py
+++ b/solution.py
@@ -32,14 +32,14 @@
     places[0, 1] = [begin, [], [take(1, EDGE)], [take(2, EDGE), take(3, EDGE)], []]
     begin = [send(1, EDGE, 0), send(1, MID, 0)] + right(1)
     places[1, 0] = [begin, [send(0, EDGE, 2), send(0, MID, 2)], [], [take(2, EDGE), take(3, EDGE)], []]
-    places[1, 1] = [begin, [send(2, EDGE, 0), send(0, EDGE, 2), send(2, MID, 0), send(3, EDGE, 0), send(0, MID, 2),
-                            send(3, MID, 0)], [], [], []]
+    places[1, 1] = [begin[:-1], [send(2, EDGE, 0), send(0, EDGE, 2), send(2, MID, 0), send(3, EDGE, 0), send(1, MID, 2),
+                                 send(0, MID, 2), send(3, MID, 0)], [], [], []]
     places[2, 0] = [[send(2, EDGE, 0), send(2, EDGE, 1), send(2, MID, 0)] + right(2),
                     [send(1, EDGE, 3), send(0, EDGE, 3), send(1, MID, 3), send(2, MID, 1), send(0, MID, 3),
                      take(3, EDGE)], [], [], []]
-    places[2, 1] = [[send(2, EDGE, 1), send(2, MID, 1)] + right(2),
-                    [send(3, EDGE, 1), send(1, EDGE, 3), send(3, MID, 1), send(0, EDGE, 3), send(1, MID, 3),
-                     send(0, MID, 3)], [], [], []]
+    places[2, 1] = [[send(2, EDGE, 1), send(2, MID, 1)] + right(2)[:-1],
+                    [send(3, EDGE, 1), send(1, EDGE, 3), send(3, MID, 1), send(0, EDGE, 3), send(2, MID, 3),
+                     send(1, MID, 3), send(0, MID, 3)], [], [], []]
     places[3, 0] = [[send(3, EDGE, 0), send(3, EDGE, 2), send(3, MID, 0), send(3, MID, 2), send(3, EDGE, 1),
                      ("load",), ("down",)], [], [take(2, EDGE), take(1, EDGE), send(3, MID, 1)], [take(0, EDGE)], []]
     places[3, 1] = [[send(3, EDGE, 2), send(3, MID, 2), ("load",), ("down",)], [], [take(2, EDGE), take(1, EDGE)],
@@ -125,15 +125,18 @@
     pieces = {EDGE: (0,), MID: (1, 2)}
     areas = [[(both, upper), (both, lower)], [(slice(0, 1), middle)], [(slice(1, 2), middle)]]
 
+    def landed(s, d, p, l):
+        return recv.at[s - jnp.where(s > d, 1, 0), p, l]
+
     def send(source, s, p, l, d, sem):
         for part, rows in areas[p]:
-            remote(source.at[l, part, rows], buf.at[s * local + l, part, rows], sent.at[sem], recv.at[s, p, l],
+            remote(source.at[l, part, rows], buf.at[s * local + l, part, rows], sent.at[sem], landed(s, d, p, l),
                    "date", d).start()
 
     def arrived(s, p, l):
         part, rows = areas[p][0] if p else (both, slice(0, 2 * HALF_ROWS))
         ref = buf.at[s * local + l, part, rows]
-        remote(ref, ref, sent.at[0], recv.at[s, p, l], "date", me).wait_recv()
+        remote(ref, ref, sent.at[0], landed(s, me, p, l), "date", me).wait_recv()
 
     def all_sent(sem, dates):
         ref = buf.at[pl.ds(0, dates)]
@@ -143,10 +146,10 @@
         return buf.at[pl.ds(s * local, local)]
 
     def rim_down(s, l):
-        return remote(buf.at[s * local + l, :, lower], top.at[s, l], rim_sent.at[0], rim_recv.at[0, s, l], "row", row + 1)
+        return remote(buf.at[s * local + l, :, lower], top.at[s, l], rim_sent.at[0], rim_recv.at[0, s], "row", row + 1)
 
     def rim_up(s, l):
-        return remote(buf.at[s * local + l, :, upper], bot.at[s, l], rim_sent.at[1], rim_recv.at[1, s, l], "row", row - 1)
+        return remote(buf.at[s * local + l, :, upper], bot.at[s, l], rim_sent.at[1], rim_recv.at[1, s], "row", row - 1)
 
     def send_rims(s, l):
         pl.when(has_down)(lambda: rim_down(s, l).start())
@@ -176,9 +179,12 @@
         col_out = lax.broadcasted_iota(jnp.int32, (width, width), 1)
         band[...] = jnp.where(jnp.abs(col_in - col_out) <= HALF_COLS, 1.0, 0.0).astype(jnp.bfloat16)
 
+    def wait_rims(s):
+        above, below = top.at[s], bot.at[s]
+        pl.when(has_up)(lambda: remote(above, above, rim_sent.at[0], rim_recv.at[0, s], "row", row).wait_recv())
+        pl.when(has_down)(lambda: remote(below, below, rim_sent.at[1], rim_recv.at[1, s], "row", row).wait_recv())
+
     def assemble(dst, s, l):
-        pl.when(has_up)(lambda: rim_down(s, l).wait_recv())
-        pl.when(has_down)(lambda: rim_up(s, l).wait_recv())
         low = height + HALF_ROWS
         for part in range(2):
             for c in range(tiles):
@@ -188,6 +194,7 @@
                 dst[part, c, low:low + HALF_ROWS] = bot[s, l, part, :, lanes]
 
     def own_dates():
+        wait_rims(me)
         for l in range(local):
             assemble(mine.at[l], me, l)
         pairs = [(i, j) for i in range(local) for j in range(i + 1, local)]
@@ -211,6 +218,8 @@
             put(j, i, real, -imag)
 
     def results(s, dates):
+        if 0 in dates:
+            wait_rims(s)
         for l in dates:
             assemble(other.at[l], s, l)
 
@@ -225,9 +234,9 @@
         held = {place: set() for place in schedule}
         shares = {place: [0, 0] for place in schedule}
 
-        def everywhere(step, *dates):
+        def everywhere(step, *places):
             for place in schedule:
-                if place[0] in dates or not dates:
+                if place in places or not places:
                     here = jnp.logical_and(me == place[0], lax.rem(row, 2) == place[1])
                     pl.when(here)(functools.partial(step, place))
 
@@ -272,17 +281,26 @@
                     for l in dates:
                         take(place, partners[place[0]][t], k, l)
 
-            @pl.when(at_end)
-            def _():
-                everywhere(functools.partial(rest, (EDGE,), range(local)), 0, n - 1)
-                for l in range(local):
-                    everywhere(functools.partial(rest, (MID,), (l,)), 0, n - 1)
-                    results(s, (l,))
-
-            @pl.when(jnp.logical_not(at_end))
-            def _():
-                everywhere(functools.partial(rest, (EDGE, MID), range(local)), *range(1, n - 1))
+            singly = jnp.logical_and(at_end, lax.rem(row, 2) == 1)
+
+            def pair():
+                everywhere(functools.partial(rest, (EDGE, MID), range(local)), *pairing)
                 results(s, tuple(range(local)))
+
+            if t < n - 2:
+                pairing = list(schedule)
+                pair()
+            else:
+                alone = [place for place in schedule if place[0] in (0, n - 1) and place[1] == 1]
+                pairing = [place for place in schedule if place not in alone]
+                pl.when(jnp.logical_not(singly))(pair)
+
+                @pl.when(singly)
+                def _():
+                    everywhere(functools.partial(rest, (EDGE,), range(local)), *alone)
+                    for l in range(local):
+                        everywhere(functools.partial(rest, (MID,), (l,)), *alone)
+                        results(s, (l,))
 
         def drain(place):
             for side, share in enumerate(shares[place]):
@@ -399,7 +417,7 @@
             pltpu.VMEM((fields, tiles, span, LANES), jnp.float32),
             pltpu.VMEM((2 * fields * height, width), jnp.bfloat16),
             dma, pltpu.SemaphoreType.REGULAR((2,)),
-            dma((n, 3, local)), dma((2,) if n == 4 else (n + 1,)), dma((2, n, local)), dma((2,)),
+            dma((n - 1, 3, local)), dma((2,) if n == 4 else (n + 1,)), dma((2, n)), dma((2,)),
         ],
         compiler_params=pltpu.CompilerParams(
             collective_id=0, has_side_effects=True,

time: 15.8 us -> 15.6 us (0.987)
  no operation moved by 1% of the time
where the time goes in v3:
time: 15.6 us; the launch traced here: 15.5 us
  Pallas kernels  15.5 us (99%)
    pallas_call x1, Pallas kernels, body(): pl.pallas_call(functools.partial(gather_kernel, n, rows_n), out_shape=kin...  14.4 us
    pallas_call x1, Pallas kernels, body(): pl.pallas_call(order_kernel, out_shape=kind, in_specs=[vmem, vmem], out_s...  1.09 us

profile of v3, /device:TPU:1, one launch (start us, length us, event | category | flops | bytes accessed | tf_op | source)
XLA Modules:
  0.0 15.5 jit_solution(12778298383948269185)
XLA Ops:
  0.0 0.0 copy-start
  0.0 14.4 %shard_map.28.coh = f32[2,8,2,16,512]{4,3,2,1,0:T(8,128)S(1)} custom-call(f32[2,2,16,512]{3,2,1,0:T(8,128)} %x_ref.1), custom_call_target="tpu_custom_call" | custom-call | tf_op jit(solution)/shard_map/pallas_call | solution.py:403
  14.4 0.0 copy-done
  14.4 1.1 %shard_map.29 = f32[2,8,2,16,512]{4,3,2,1,0:T(8,128)} custom-call(s32[8]{0:T(128)S(1)} %copy-done, f32[2,8,2,16,512]{4,3,2,1,0:T(8,128)S(1)} %shard_map.28.coh), custom_call_target="tpu_custom_call" | custom-call | tf_op jit(solution)/shard_map/pallas_call | solution.py:426
Async XLA Ops:
  0.0 14.4 %copy-start = (s32[8]{0:T(128)S(1)}, s32[8]{0:T(128)}, u32[]{:S(2)}) copy-start(s32[8]{0:T(128)} %plan_ref.1) | copy-start | bytes 100

commit v4 on v3

--- a/solution.py
+++ b/solution.py
@@ -40,8 +40,9 @@
     places[2, 1] = [[send(2, EDGE, 1), send(2, MID, 1)] + right(2)[:-1],
                     [send(3, EDGE, 1), send(1, EDGE, 3), send(3, MID, 1), send(0, EDGE, 3), send(2, MID, 3),
                      send(1, MID, 3), send(0, MID, 3)], [], [], []]
-    places[3, 0] = [[send(3, EDGE, 0), send(3, EDGE, 2), send(3, MID, 0), send(3, MID, 2), send(3, EDGE, 1),
-                     ("load",), ("down",)], [], [take(2, EDGE), take(1, EDGE), send(3, MID, 1)], [take(0, EDGE)], []]
+    places[3, 0] = [[send(3, EDGE, 0), send(3, EDGE, 2), send(3, MID, 0), send(3, MID, 2), ("lower", 3, EDGE, 1),
+                     ("load",), ("down",)], [], [take(2, EDGE), ("upper", 3, EDGE, 1), take(1, EDGE), send(3, MID, 1)],
+                    [take(0, EDGE)], []]
     places[3, 1] = [[send(3, EDGE, 2), send(3, MID, 2), ("load",), ("down",)], [], [take(2, EDGE), take(1, EDGE)],
                     [take(0, EDGE)], []]
     return places, {0: (1, 2, 3), 1: (0, 2, 3), 2: (1, 0, 3), 3: (2, 1, 0)}
@@ -55,6 +56,7 @@
     count = len(fields)
     _, tiles, span, _ = pbuf.shape
     height = span - 2 * HALF_ROWS
+    blocks, rows, half = tiles // 2, 2 * count * height, count * height
     for f, field in enumerate(fields):
         pbuf[f] = field
     for f in range(count):
@@ -63,12 +65,28 @@
         total = (sbuf[f, :, 0:height] + sbuf[f, :, 3:height + 3]) + sbuf[f, :, 6:height + 6]
         high = total.astype(jnp.bfloat16)
         low = (total - high.astype(jnp.float32)).astype(jnp.bfloat16)
-        for c in range(tiles):
-            lhs[f * height:(f + 1) * height, c * LANES:(c + 1) * LANES] = high[c]
-            lhs[(count + f) * height:(count + f + 1) * height, c * LANES:(c + 1) * LANES] = low[c]
-    sums = jnp.dot(lhs[0:2 * count * height], band[...], preferred_element_type=jnp.float32)
-    return [sums[f * height:(f + 1) * height] + sums[(count + f) * height:(count + f + 1) * height]
-            for f in range(count)]
+        for first, values in ((f * height, high), (half + f * height, low)):
+            for c in range(tiles):
+                block, side = c // 2, c % 2
+                lhs[block * rows + first:block * rows + first + height, side * LANES:(side + 1) * LANES] = values[c]
+                seam = (c - 1) // 2
+                if 0 < c < tiles - 1:
+                    start = (blocks + seam) * rows + first
+                    lhs[start:start + height, (1 - side) * LANES:(2 - side) * LANES] = values[c]
+    main = jnp.dot(lhs[0:blocks * rows], band[0:2 * LANES], preferred_element_type=jnp.float32)
+    seams = jnp.dot(lhs[blocks * rows:(2 * blocks - 1) * rows], band[2 * LANES:4 * LANES], preferred_element_type=jnp.float32)
+    columns = []
+    for c in range(tiles):
+        block, side = c // 2, c % 2
+        lanes = slice(side * LANES, (side + 1) * LANES)
+        value = main[block * rows:block * rows + half, lanes] + main[block * rows + half:(block + 1) * rows, lanes]
+        if 0 < c < tiles - 1:
+            start = (c - 1) // 2 * rows
+            lanes = slice((1 - side) * LANES, (2 - side) * LANES)
+            value = value + (seams[start:start + half, lanes] + seams[start + half:start + rows, lanes])
+        columns.append(value)
+    sums = jnp.concatenate(columns, axis=1)
+    return [sums[f * height:(f + 1) * height] for f in range(count)]
 
 
 def partner_results(mine, other, pw, dates, put, band, *work):
@@ -175,9 +193,13 @@
         def _():
             bot[...] = jnp.zeros_like(bot)
 
-        col_in = lax.broadcasted_iota(jnp.int32, (width, width), 0)
-        col_out = lax.broadcasted_iota(jnp.int32, (width, width), 1)
-        band[...] = jnp.where(jnp.abs(col_in - col_out) <= HALF_COLS, 1.0, 0.0).astype(jnp.bfloat16)
+        size = 2 * LANES
+        col_in = lax.broadcasted_iota(jnp.int32, (size, size), 0)
+        col_out = lax.broadcasted_iota(jnp.int32, (size, size), 1)
+        near = jnp.abs(col_in - col_out) <= HALF_COLS
+        across = jnp.logical_and(near, jnp.logical_xor(col_in < LANES, col_out < LANES))
+        band[0:size] = jnp.where(near, 1.0, 0.0).astype(jnp.bfloat16)
+        band[size:2 * size] = jnp.where(across, 1.0, 0.0).astype(jnp.bfloat16)
 
     def wait_rims(s):
         above, below = top.at[s], bot.at[s]
@@ -257,6 +279,15 @@
                         for p in pieces[k]:
                             send(x_ref if s == place[0] and d < s else dates_of(s), s, p, l, d, int(d > place[0]))
                         shares[place][d > place[0]] += 1
+                elif op in ("upper", "lower"):
+                    s, k, d = rest
+
+                    @pl.when((row < rows_n // 2) if op == "upper" else (row >= rows_n // 2))
+                    def _():
+                        for l in range(local):
+                            for p in pieces[k]:
+                                send(x_ref, s, p, l, d, 0)
+                    shares[place][0] += local if op == "upper" else 0
                 elif op == "take":
                     for l in range(local):
                         take(place, *rest, l)
@@ -409,13 +440,13 @@
             pltpu.VMEM((local, 2, tiles, span, LANES), jnp.float32),
             pltpu.VMEM((local, 2, tiles, span, LANES), jnp.float32),
             pltpu.VMEM((local, height, width), jnp.float32),
-            pltpu.VMEM((width, width), jnp.bfloat16),
+            pltpu.VMEM((4 * LANES, 2 * LANES), jnp.bfloat16),
             pltpu.VMEM((n * local, 2, height, width), jnp.float32),
             pltpu.VMEM((n, local, 2, HALF_ROWS, width), jnp.float32),
             pltpu.VMEM((n, local, 2, HALF_ROWS, width), jnp.float32),
             pltpu.VMEM((fields, tiles, span, LANES), jnp.float32),
             pltpu.VMEM((fields, tiles, span, LANES), jnp.float32),
-            pltpu.VMEM((2 * fields * height, width), jnp.bfloat16),
+            pltpu.VMEM((2 * fields * height * (tiles - 1), 2 * LANES), jnp.bfloat16),
             dma, pltpu.SemaphoreType.REGULAR((2,)),
             dma((n - 1, 3, local)), dma((2,) if n == 4 else (n + 1,)), dma((2, n)), dma((2,)),
         ],

time: 15.6 us -> 15.4 us (0.987)
  the two profiles are of different devices: /device:TPU:1 before, /device:TPU:25 now
where the time goes in v4:
time: 15.4 us; the launch traced here: 15.3 us
  Pallas kernels  15.3 us (99%)
    pallas_call x1, Pallas kernels, body(): pl.pallas_call(functools.partial(gather_kernel, n, rows_n), out_shape=kin...  14.2 us
    pallas_call x1, Pallas kernels, body(): pl.pallas_call(order_kernel, out_shape=kind, in_specs=[vmem, vmem], out_s...  1.09 us

profile of v4, /device:TPU:25, one launch (start us, length us, event | category | flops | bytes accessed | tf_op | source)
XLA Modules:
  0.0 15.3 jit_solution(6197816023369471812)
XLA Ops:
  0.0 0.0 copy-start
  0.0 14.2 %shard_map.28.coh = f32[2,8,2,16,512]{4,3,2,1,0:T(8,128)S(1)} custom-call(f32[2,2,16,512]{3,2,1,0:T(8,128)} %x_ref.1), custom_call_target="tpu_custom_call" | custom-call | tf_op jit(solution)/shard_map/pallas_call | solution.py:434
  14.2 0.0 copy-done
  14.2 1.1 %shard_map.29 = f32[2,8,2,16,512]{4,3,2,1,0:T(8,128)} custom-call(s32[8]{0:T(128)S(1)} %copy-done, f32[2,8,2,16,512]{4,3,2,1,0:T(8,128)S(1)} %shard_map.28.coh), custom_call_target="tpu_custom_call" | custom-call | tf_op jit(solution)/shard_map/pallas_call | solution.py:457
Async XLA Ops:
  0.0 14.2 %copy-start = (s32[8]{0:T(128)S(1)}, s32[8]{0:T(128)}, u32[]{:S(2)}) copy-start(s32[8]{0:T(128)} %plan_ref.1) | copy-start | bytes 100

commit v5 on v4

--- a/solution.py
+++ b/solution.py
@@ -140,8 +140,8 @@
     upper, lower = slice(0, HALF_ROWS), slice(height - HALF_ROWS, height)
     middle = slice(HALF_ROWS, height - HALF_ROWS)
     both = slice(0, 2)
-    pieces = {EDGE: (0,), MID: (1, 2)}
-    areas = [[(both, upper), (both, lower)], [(slice(0, 1), middle)], [(slice(1, 2), middle)]]
+    pieces = {EDGE: (0,), MID: (1,)}
+    areas = [[(both, upper), (both, lower)], [(both, middle)]]
 
     def landed(s, d, p, l):
         return recv.at[s - jnp.where(s > d, 1, 0), p, l]
@@ -312,7 +312,7 @@
                     for l in dates:
                         take(place, partners[place[0]][t], k, l)
 
-            singly = jnp.logical_and(at_end, lax.rem(row, 2) == 1)
+            singly = jnp.logical_and(me == 0, lax.rem(row, 2) == 1)
 
             def pair():
                 everywhere(functools.partial(rest, (EDGE, MID), range(local)), *pairing)
@@ -322,7 +322,7 @@
                 pairing = list(schedule)
                 pair()
             else:
-                alone = [place for place in schedule if place[0] in (0, n - 1) and place[1] == 1]
+                alone = [place for place in schedule if place == (0, 1)]
                 pairing = [place for place in schedule if place not in alone]
                 pl.when(jnp.logical_not(singly))(pair)
 
@@ -448,7 +448,7 @@
             pltpu.VMEM((fields, tiles, span, LANES), jnp.float32),
             pltpu.VMEM((2 * fields * height * (tiles - 1), 2 * LANES), jnp.bfloat16),
             dma, pltpu.SemaphoreType.REGULAR((2,)),
-            dma((n - 1, 3, local)), dma((2,) if n == 4 else (n + 1,)), dma((2, n)), dma((2,)),
+            dma((n - 1, 2, local)), dma((2,) if n == 4 else (n + 1,)), dma((2, n)), dma((2,)),
         ],
         compiler_params=pltpu.CompilerParams(
             collective_id=0, has_side_effects=True,

time: 15.4 us -> 15.2 us (0.987)
  the two profiles are of different devices: /device:TPU:25 before, /device:TPU:1 now
where the time goes in v5:
time: 15.2 us; the launch traced here: 15 us
  Pallas kernels  15 us (99%)
    pallas_call x1, Pallas kernels, body(): pl.pallas_call(functools.partial(gather_kernel, n, rows_n), out_shape=kin...  13.9 us
    pallas_call x1, Pallas kernels, body(): pl.pallas_call(order_kernel, out_shape=kind, in_specs=[vmem, vmem], out_s...  1.09 us

profile of v5, /device:TPU:1, one launch (start us, length us, event | category | flops | bytes accessed | tf_op | source)
XLA Modules:
  0.0 15.0 jit_solution(9450837387311641640)
XLA Ops:
  0.0 0.0 copy-start
  0.0 13.9 %shard_map.28.coh = f32[2,8,2,16,512]{4,3,2,1,0:T(8,128)S(1)} custom-call(f32[2,2,16,512]{3,2,1,0:T(8,128)} %x_ref.1), custom_call_target="tpu_custom_call" | custom-call | tf_op jit(solution)/shard_map/pallas_call | solution.py:434
  13.9 0.0 copy-done
  13.9 1.1 %shard_map.29 = f32[2,8,2,16,512]{4,3,2,1,0:T(8,128)} custom-call(s32[8]{0:T(128)S(1)} %copy-done, f32[2,8,2,16,512]{4,3,2,1,0:T(8,128)S(1)} %shard_map.28.coh), custom_call_target="tpu_custom_call" | custom-call | tf_op jit(solution)/shard_map/pallas_call | solution.py:457
Async XLA Ops:
  0.0 13.9 %copy-start = (s32[8]{0:T(128)S(1)}, s32[8]{0:T(128)}, u32[]{:S(2)}) copy-start(s32[8]{0:T(128)} %plan_ref.1) | copy-start | bytes 100

commit v6 on v5

--- a/solution.py
+++ b/solution.py
@@ -32,13 +32,14 @@
     places[0, 1] = [begin, [], [take(1, EDGE)], [take(2, EDGE), take(3, EDGE)], []]
     begin = [send(1, EDGE, 0), send(1, MID, 0)] + right(1)
     places[1, 0] = [begin, [send(0, EDGE, 2), send(0, MID, 2)], [], [take(2, EDGE), take(3, EDGE)], []]
-    places[1, 1] = [begin[:-1], [send(2, EDGE, 0), send(0, EDGE, 2), send(2, MID, 0), send(3, EDGE, 0), send(1, MID, 2),
+    places[1, 1] = [begin[:-1] + [("upper", 1, MID, 2)],
+                    [send(2, EDGE, 0), send(0, EDGE, 2), send(2, MID, 0), send(3, EDGE, 0), ("lower", 1, MID, 2),
                                  send(0, MID, 2), send(3, MID, 0)], [], [], []]
     places[2, 0] = [[send(2, EDGE, 0), send(2, EDGE, 1), send(2, MID, 0)] + right(2),
                     [send(1, EDGE, 3), send(0, EDGE, 3), send(1, MID, 3), send(2, MID, 1), send(0, MID, 3),
                      take(3, EDGE)], [], [], []]
-    places[2, 1] = [[send(2, EDGE, 1), send(2, MID, 1)] + right(2)[:-1],
-                    [send(3, EDGE, 1), send(1, EDGE, 3), send(3, MID, 1), send(0, EDGE, 3), send(2, MID, 3),
+    places[2, 1] = [[send(2, EDGE, 1), send(2, MID, 1)] + right(2)[:-1] + [("upper", 2, MID, 3)],
+                    [send(3, EDGE, 1), send(1, EDGE, 3), send(3, MID, 1), send(0, EDGE, 3), ("lower", 2, MID, 3),
                      send(1, MID, 3), send(0, MID, 3)], [], [], []]
     places[3, 0] = [[send(3, EDGE, 0), send(3, EDGE, 2), send(3, MID, 0), send(3, MID, 2), ("lower", 3, EDGE, 1),
                      ("load",), ("down",)], [], [take(2, EDGE), ("upper", 3, EDGE, 1), take(1, EDGE), send(3, MID, 1)],
@@ -286,8 +287,8 @@
                     def _():
                         for l in range(local):
                             for p in pieces[k]:
-                                send(x_ref, s, p, l, d, 0)
-                    shares[place][0] += local if op == "upper" else 0
+                                send(x_ref if d < s else dates_of(s), s, p, l, d, int(d > s))
+                    shares[place][d > s] += local if op == "upper" else 0
                 elif op == "take":
                     for l in range(local):
                         take(place, *rest, l)

time: 15.2 us -> 15.3 us (level)
  the two profiles are of different devices: /device:TPU:1 before, /device:TPU:12 now
where the time goes in v6:
time: 15.3 us; the launch traced here: 15.2 us
  Pallas kernels  15.2 us (99%)
    pallas_call x1, Pallas kernels, body(): pl.pallas_call(functools.partial(gather_kernel, n, rows_n), out_shape=kin...  14.1 us
    pallas_call x1, Pallas kernels, body(): pl.pallas_call(order_kernel, out_shape=kind, in_specs=[vmem, vmem], out_s...  1.09 us

profile of v6, /device:TPU:12, one launch (start us, length us, event | category | flops | bytes accessed | tf_op | source)
XLA Modules:
  0.0 15.2 jit_solution(2183693374020687959)
XLA Ops:
  0.0 0.0 copy-start
  0.0 14.1 %shard_map.28.coh = f32[2,8,2,16,512]{4,3,2,1,0:T(8,128)S(1)} custom-call(f32[2,2,16,512]{3,2,1,0:T(8,128)} %x_ref.1), custom_call_target="tpu_custom_call" | custom-call | tf_op jit(solution)/shard_map/pallas_call | solution.py:435
  14.1 0.0 copy-done
  14.1 1.1 %shard_map.29 = f32[2,8,2,16,512]{4,3,2,1,0:T(8,128)} custom-call(s32[8]{0:T(128)S(1)} %copy-done, f32[2,8,2,16,512]{4,3,2,1,0:T(8,128)S(1)} %shard_map.28.coh), custom_call_target="tpu_custom_call" | custom-call | tf_op jit(solution)/shard_map/pallas_call | solution.py:458
Async XLA Ops:
  0.0 14.1 %copy-start = (s32[8]{0:T(128)S(1)}, s32[8]{0:T(128)}, u32[]{:S(2)}) copy-start(s32[8]{0:T(128)} %plan_ref.1) | copy-start | bytes 100
